TPU v7x, 512 devices: a whole 4x4x16 slice. The times are simulated.
512 devices in a mesh: ctx: 64 (over z_hi, x, y), head: 8 (over z_lo, core).
Axes of the slice: x: 4, y: 4, z: 16 (z_hi: 4, z_lo: 4; z = z_hi * 4 + z_lo), core: 2. Of those that a mesh axis runs over, the one named last changes fastest.
Arguments:
- queries: bfloat16 [16384, 6144], P(('ctx', 'head')), may hold values from -32 to 32
- keys: bfloat16 [16384, 6144], P(('ctx', 'head')), may hold values from -12 to 12
- values: bfloat16 [16384, 6144], P(('ctx', 'head')), may hold values from -6 to 6
- cache_keys: bfloat16 [32768, 6144], P('ctx', 'head'), may hold values from -6 to 6
- cache_values: bfloat16 [32768, 6144], P('ctx', 'head'), may hold values from -6 to 6
- pattern: int32 [128, 4], replicated, may hold values from 0 to 255, as said below
- reached: int32 [128], replicated, may hold values from 1 to 4, as said below
- gate: float32 [6144], replicated, may hold values from 0.5 to 2
Outputs:
- mixed: bfloat16 [16384, 6144], P(('ctx', 'head'))
Inputs may be any that keep to these rules, and one draw needn't show every extreme that they name: `pattern`: every entry of row g names a cached tile of ctx index g // 2 - 1, g // 2 or g // 2 + 1, where ctx index c holds cached tiles c * 4 to (c + 1) * 4 - 1. Only the first reached[g] entries of row g of pattern are used.
All inputs are finite; a program needn't handle non-finite values.
Results may differ from a plain program's by a relative error of at most 0.011.
Values may be sent and summed in bfloat16 or wider, within the bound.
No kernel may reach another device: no remote copies, remote signals or barrier semaphores. Data moves between devices by JAX's collectives and lax.ppermute only.
A program may use at most 64 MiB of HBM per device.

v0:
```python
import jax
import jax.numpy as jnp
from jax import lax
from jax.sharding import PartitionSpec as P

HD = 128
TILE = 128
REACH = 4
NEGATIVE = -1e30


def with_halo(block, sides, width):
    for axis, dim in sides:
        count = lax.axis_size(axis)
        forward = [(i, i + 1) for i in range(count - 1)]
        backward = [(target, source) for source, target in forward]
        low = lax.ppermute(
            lax.slice_in_dim(block, block.shape[dim] - width, None, axis=dim), axis, forward
        )
        high = lax.ppermute(lax.slice_in_dim(block, 0, width, axis=dim), axis, backward)
        block = jnp.concatenate([low, block, high], axis=dim)
    return block


def tile_attend(q_tile, key_blocks, value_blocks, usable_keys):
    scores = jnp.einsum(
        "qhd,nkhd->hqnk", q_tile, key_blocks, preferred_element_type=jnp.float32
    ) * q_tile.shape[2] ** (-0.5)
    keep_mask = usable_keys[None, None, :, None]
    scores = jnp.where(keep_mask, scores, NEGATIVE)
    row_peak = jnp.max(scores, axis=(2, 3))
    expos = jnp.exp(scores - row_peak[:, :, None, None])
    row_total = jnp.sum(expos, axis=(2, 3))
    weights = expos.astype(jnp.bfloat16)
    summed = jnp.einsum("hqnk,nkhd->qhd", weights, value_blocks, preferred_element_type=jnp.float32)
    return (summed, row_peak, row_total)


def finish(portions):
    overall_peak = portions[0][1]
    numerator = 0.0
    denominator = 0.0
    for portion in portions:
        factor = jnp.exp(portion[1] - overall_peak)
        denominator = denominator + factor * portion[2]
        numerator = numerator + portion[0] * jnp.transpose(factor, (0, 2, 1))[..., None]
    return numerator / jnp.transpose(denominator, (0, 2, 1))[..., None]


def local(queries, keys, values, cache_keys, cache_values, pattern, reached, gate):
    local_q, local_k, local_v = (
        lax.all_to_all(queries, "head", split_axis=1, concat_axis=0, tiled=True),
        lax.all_to_all(keys, "head", split_axis=1, concat_axis=0, tiled=True),
        lax.all_to_all(values, "head", split_axis=1, concat_axis=0, tiled=True),
    )
    rows = local_q.shape[0]
    width = local_q.shape[1]
    heads_here = width // HD
    tiles_here = rows // TILE
    ctx_count = lax.axis_size("ctx")
    ctx_index = lax.axis_index("ctx")
    all_tiles = ctx_count * tiles_here
    first_tile = ctx_index * tiles_here
    cache_tiles = cache_keys.shape[0] // TILE
    rim_blocks = with_halo(jnp.stack([local_k, local_v]), (("ctx", 1),), 2 * TILE)
    tile_ids = first_tile + jnp.arange(tiles_here, dtype=jnp.int32)
    near_ids = tile_ids[:, None] + jnp.arange(-2, 3, dtype=jnp.int32)[None, :]
    group_valid = (near_ids >= 0) & (near_ids < all_tiles)
    own_pattern = lax.dynamic_slice_in_dim(pattern, first_tile, tiles_here, 0)
    own_reached = lax.dynamic_slice_in_dim(reached, first_tile, tiles_here, 0)
    slot_ids = jnp.arange(REACH, dtype=jnp.int32)
    cache_stack = jnp.stack([cache_keys, cache_values])

    def query_tile(block_q, tile_index):
        return lax.dynamic_slice_in_dim(block_q, tile_index * TILE, TILE, 0).reshape(
            TILE, heads_here, HD
        )

    def group_blocks(tile_index):
        window = lax.dynamic_slice_in_dim(rim_blocks, tile_index * TILE, 5 * TILE, 1)
        return window.reshape(2, 5, TILE, heads_here, HD)

    widened = with_halo(cache_stack, (("ctx", 1),), cache_keys.shape[0])
    widened = widened.reshape(2, 3 * cache_tiles, TILE, heads_here, HD)

    def one_tile(tile_index):
        local_ids = own_pattern[tile_index] - (ctx_index - 1) * cache_tiles
        picked = jnp.take(widened, local_ids, axis=1)
        blocks = jnp.concatenate([group_blocks(tile_index), picked], axis=1)
        usable_keys = jnp.concatenate([group_valid[tile_index], slot_ids < own_reached[tile_index]])
        return tile_attend(query_tile(local_q, tile_index), blocks[0], blocks[1], usable_keys)

    attended = finish([lax.map(one_tile, jnp.arange(tiles_here, dtype=jnp.int32))])
    gate_part = lax.dynamic_slice_in_dim(gate, lax.axis_index("head") * width, width, 0)
    gated = (attended.reshape(rows, width) * gate_part).astype(jnp.bfloat16)
    return lax.all_to_all(gated, "head", split_axis=0, concat_axis=1, tiled=True)


def solution(mesh):
    placed = (
        P(("ctx", "head"), None),
        P(("ctx", "head"), None),
        P(("ctx", "head"), None),
        P("ctx", "head"),
        P("ctx", "head"),
        P(),
        P(),
        P(),
    )
    return jax.shard_map(
        local, mesh=mesh, in_specs=placed, out_specs=P(("ctx", "head"), None), check_vma=False
    )
```

profile of v0, /device:TPU:256, one launch (start us, length us, event | category | flops | bytes accessed | tf_op | source)
XLA Modules:
  0.0 328.4 jit_solution(431748586827617101)
XLA Ops:
  0.0 1.9 copy.82
  1.9 3.6 %all-to-all-start = ((bf16[32,8,768]{2,0,1:T(8,128)(2,1)}), bf16[32,8,768]{2,0,1:T(8,128)(2,1)S(1)}, u32[]{:S(2)}, u32[]{:S(2)}) async-start(bf16[32,8,768]{2,0,1:T(8,128)(2,1)} %bitcast.70), calls=%async_computation | async-start | bytes 786432 | tf_op jit(solution)/shard_map/all_to_all | solution.py:53
  5.5 1.8 copy.81
  7.3 10.7 %all-to-all-done = bf16[32,8,768]{2,0,1:T(8,128)(2,1)S(1)} async-done(((bf16[32,8,768]{2,0,1:T(8,128)(2,1)}), bf16[32,8,768]{2,0,1:T(8,128)(2,1)S(1)}, u32[]{:S(2)}, u32[]{:S(2)}) %all-to-all-start) | async-done | bytes 393248 | tf_op jit(solution)/shard_map/all_to_all | solution.py:53
  18.0 3.5 %all-to-all-start.1 = ((bf16[32,8,768]{2,0,1:T(8,128)(2,1)}), bf16[32,8,768]{2,0,1:T(8,128)(2,1)S(1)}, u32[]{:S(2)}, u32[]{:S(2)}) async-start(bf16[32,8,768]{2,0,1:T(8,128)(2,1)} %bitcast.69), calls=%async_computation.1 | async-start | bytes 786432 | tf_op jit(solution)/shard_map/all_to_all | solution.py:54
  22.8 3.5 %collective-permute-start.2 = (bf16[2,512,768]{2,1,0:T(8,128)(2,1)}, bf16[2,512,768]{2,1,0:T(8,128)(2,1)}, u32[]{:S(2)}, u32[]{:S(2)}) collective-permute-start(bf16[2,512,768]{2,1,0:T(8,128)(2,1)} %pad_maximum_fusion.3), channel_id=1, source_target_pairs={{0,8},{8,16},{16,24},{24,32},{32,40},{40,48},{48,56},{56,64},{64,7... | collective-permute-start | bytes 4718600 | tf_op jit(solution)/shard_map/ppermute | solution.py:17
  26.2 10.5 %collective-permute-start.3 = (bf16[2,512,768]{2,1,0:T(8,128)(2,1)}, bf16[2,512,768]{2,1,0:T(8,128)(2,1)}, u32[]{:S(2)}, u32[]{:S(2)}) collective-permute-start(bf16[2,512,768]{2,1,0:T(8,128)(2,1)} %pad_maximum_fusion.3), channel_id=1, source_target_pairs={{8,0},{16,8},{24,16},{32,24},{40,32},{48,40},{56,48},{64,56},{72,6... | collective-permute-start | bytes 4718600 | tf_op jit(solution)/shard_map/ppermute | solution.py:20
  37.5 5.0 %all-to-all-start.2 = ((bf16[32,8,768]{2,0,1:T(8,128)(2,1)}), bf16[32,8,768]{2,0,1:T(8,128)(2,1)S(1)}, u32[]{:S(2)}, u32[]{:S(2)}) async-start(bf16[32,8,768]{2,0,1:T(8,128)(2,1)} %bitcast.68), calls=%async_computation.2 | async-start | bytes 786432 | tf_op jit(solution)/shard_map/all_to_all | solution.py:52
  44.6 1.9 collective-permute-start
  46.5 37.1 %collective-permute-start.1 = (bf16[2,256,768]{2,1,0:T(8,128)(2,1)}, bf16[2,256,768]{2,1,0:T(8,128)(2,1)}, u32[]{:S(2)}, u32[]{:S(2)}) collective-permute-start(bf16[2,256,768]{2,1,0:T(8,128)(2,1)} %pad_maximum_fusion.4), channel_id=1, source_target_pairs={{8,0},{16,8},{24,16},{32,24},{40,32},{48,40},{56,48},{64,56},{72,6... | collective-permute-start | bytes 2359304 | tf_op jit(solution)/shard_map/ppermute | solution.py:20
  83.7 128.9 %collective-permute-done.3 = bf16[2,512,768]{2,1,0:T(8,128)(2,1)} collective-permute-done((bf16[2,512,768]{2,1,0:T(8,128)(2,1)}, bf16[2,512,768]{2,1,0:T(8,128)(2,1)}, u32[]{:S(2)}, u32[]{:S(2)}) %collective-permute-start.3) | collective-permute-done | bytes 1572896 | tf_op jit(solution)/shard_map/ppermute | solution.py:20
  212.6 4.9 %pad_maximum_fusion.1 = bf16[2,1536,768]{2,1,0:T(8,128)(2,1)} fusion(bf16[2,512,768]{2,1,0:T(8,128)(2,1)} %collective-permute-done.3, bf16[1,512,768]{2,1,0:T(8,128)(2,1)S(1)} %bitcast.112, bf16[1,512,768]{2,1,0:T(8,128)(2,1)S(1)} %bitcast.114, bf16[2,512,768]{2,1,0:T(8,128)(2,1)} %collective-permute-done.2), kind=kLoop, calls=%fused_computation.38 | loop fusion | flops 18874368 | bytes 9437184 | tf_op jit(solution)/shard_map/concatenate | solution.py:21
  217.5 10.8 %reshape.82 = bf16[2,12,128,6,128]{4,3,2,1,0:T(8,128)(2,1)} reshape(bf16[2,1536,768]{2,1,0:T(8,128)(2,1)} %pad_maximum_fusion.1) | data formatting | bytes 9437184 | tf_op jit(solution)/shard_map/reshape | solution.py:84
  228.3 6.4 %copy.60 = bf16[2,12,128,6,128]{4,2,3,1,0:T(8,128)(2,1)} copy(bf16[2,12,128,6,128]{4,3,2,1,0:T(8,128)(2,1)} %reshape.82) | data formatting | bytes 9437184
  234.7 13.2 %collective-permute-done = bf16[2,256,768]{2,1,0:T(8,128)(2,1)} collective-permute-done((bf16[2,256,768]{2,1,0:T(8,128)(2,1)}, bf16[2,256,768]{2,1,0:T(8,128)(2,1)}, u32[]{:S(2)}, u32[]{:S(2)}) %collective-permute-start) | collective-permute-done | bytes 786464 | tf_op jit(solution)/shard_map/ppermute | solution.py:17
  247.9 3.0 pad_maximum_fusion.2
  250.9 47.6 %while.17 = (s32[]{:T(128)}, f32[2,128,6,128]{1,3,2,0:T(8,128)}, f32[2,6,128]{2,1,0:T(8,128)S(1)}, f32[2,6,128]{2,1,0:T(8,128)S(1)}, s32[2]{0:T(128)S(1)}, /*ind...) while((s32[]{:T(128)}, f32[2,128,6,128]{1,3,2,0:T(8,128)}, ...), condition=%wide.region_3.4_spmd.clone, body=%wide.region_0.3_spmd.clone.sunk | while | flops 465272384 | bytes 78874744 | solution.py:93
  253.6 3.2 gather_fusion
  258.9 2.9 constant_dynamic-slice_fusion.6
  261.9 4.2 %reshape.105 = bf16[2,5,128,6,128]{4,3,2,1,0:T(8,128)(2,1)S(1)} reshape(bf16[2,640,768]{2,1,0:T(8,128)(2,1)} %constant_dynamic-slice_fusion.6) | data formatting | bytes 3932160 | tf_op jit(solution)/shard_map/while/body/eval_jaxpr/reshape | solution.py:81
  277.4 3.2 gather_fusion
  282.7 2.9 constant_dynamic-slice_fusion.6
  285.7 4.2 %reshape.105 = bf16[2,5,128,6,128]{4,3,2,1,0:T(8,128)(2,1)S(1)} reshape(bf16[2,640,768]{2,1,0:T(8,128)(2,1)} %constant_dynamic-slice_fusion.6) | data formatting | bytes 3932160 | tf_op jit(solution)/shard_map/while/body/eval_jaxpr/reshape | solution.py:81
  300.4 27.2 %all_to_all.67 = bf16[8,32,768]{2,1,0:T(8,128)(2,1)S(1)} all-to-all(bf16[8,32,768]{2,1,0:T(8,128)(2,1)S(1)} %multiply_convert_fusion), channel_id=1, replica_groups=mesh['ctx'=64,'head'=8] {'head'}, dimensions={0} | all-to-all | bytes 786432 | tf_op jit(solution)/shard_map/all_to_all | solution.py:96
  (94 shorter events, 28.0 us)
Async XLA Ops:
  0.0 42.5 %copy-start = (s32[128,4]{0,1:T(4,128)S(1)}, s32[128,4]{0,1:T(4,128)}, u32[]{:S(2)}) copy-start(s32[128,4]{0,1:T(4,128)} %param.15) | copy-start | bytes 6148
  0.0 21.4 %copy-start.6 = (bf16[512,768]{1,0:T(8,128)(2,1)S(1)}, bf16[512,768]{1,0:T(8,128)(2,1)}, u32[]{:S(2)}) copy-start(bf16[512,768]{1,0:T(8,128)(2,1)} %param.13) | copy-start | bytes 2359300
  0.0 21.4 %copy-start.5 = (bf16[512,768]{1,0:T(8,128)(2,1)S(1)}, bf16[512,768]{1,0:T(8,128)(2,1)}, u32[]{:S(2)}) copy-start(bf16[512,768]{1,0:T(8,128)(2,1)} %param.14) | copy-start | bytes 2359300
  0.0 36.7 %copy-start.9 = (bf16[32,6144]{1,0:T(8,128)(2,1)S(1)}, bf16[32,6144]{1,0:T(8,128)(2,1)}, u32[]{:S(2)}) copy-start(bf16[32,6144]{1,0:T(8,128)(2,1)} %param.10) | copy-start | bytes 1179652
  1.9 40.8 %copy-start.10 = (s32[128]{0:T(128)S(1)}, s32[128]{0:T(128)}, u32[]{:S(2)}) copy-start(s32[128]{0:T(128)} %param.16) | copy-start | bytes 1540
  1.9 16.0 %all-to-all-start = ((bf16[32,8,768]{2,0,1:T(8,128)(2,1)}), bf16[32,8,768]{2,0,1:T(8,128)(2,1)S(1)}, u32[]{:S(2)}, u32[]{:S(2)}) async-start(bf16[32,8,768]{2,0,1:T(8,128)(2,1)} %bitcast.70), calls=%async_computation | async-start | bytes 786432 | tf_op jit(solution)/shard_map/all_to_all | solution.py:53
  18.0 19.5 %all-to-all-start.1 = ((bf16[32,8,768]{2,0,1:T(8,128)(2,1)}), bf16[32,8,768]{2,0,1:T(8,128)(2,1)S(1)}, u32[]{:S(2)}, u32[]{:S(2)}) async-start(bf16[32,8,768]{2,0,1:T(8,128)(2,1)} %bitcast.69), calls=%async_computation.1 | async-start | bytes 786432 | tf_op jit(solution)/shard_map/all_to_all | solution.py:54
  22.8 60.9 %collective-permute-start.2 = (bf16[2,512,768]{2,1,0:T(8,128)(2,1)}, bf16[2,512,768]{2,1,0:T(8,128)(2,1)}, u32[]{:S(2)}, u32[]{:S(2)}) collective-permute-start(bf16[2,512,768]{2,1,0:T(8,128)(2,1)} %pad_maximum_fusion.3), channel_id=1, source_target_pairs={{0,8},{8,16},{16,24},{24,32},{32,40},{40,48},{48,56},{56,64},{64,7... | collective-permute-start | bytes 4718600 | tf_op jit(solution)/shard_map/ppermute | solution.py:17
  26.2 186.4 %collective-permute-start.3 = (bf16[2,512,768]{2,1,0:T(8,128)(2,1)}, bf16[2,512,768]{2,1,0:T(8,128)(2,1)}, u32[]{:S(2)}, u32[]{:S(2)}) collective-permute-start(bf16[2,512,768]{2,1,0:T(8,128)(2,1)} %pad_maximum_fusion.3), channel_id=1, source_target_pairs={{8,0},{16,8},{24,16},{32,24},{40,32},{48,40},{56,48},{64,56},{72,6... | collective-permute-start | bytes 4718600 | tf_op jit(solution)/shard_map/ppermute | solution.py:20
  37.5 213.4 %all-to-all-start.2 = ((bf16[32,8,768]{2,0,1:T(8,128)(2,1)}), bf16[32,8,768]{2,0,1:T(8,128)(2,1)S(1)}, u32[]{:S(2)}, u32[]{:S(2)}) async-start(bf16[32,8,768]{2,0,1:T(8,128)(2,1)} %bitcast.68), calls=%async_computation.2 | async-start | bytes 786432 | tf_op jit(solution)/shard_map/all_to_all | solution.py:52
  44.6 203.4 %collective-permute-start = (bf16[2,256,768]{2,1,0:T(8,128)(2,1)}, bf16[2,256,768]{2,1,0:T(8,128)(2,1)}, u32[]{:S(2)}, u32[]{:S(2)}) collective-permute-start(bf16[2,256,768]{2,1,0:T(8,128)(2,1)} %pad_maximum_fusion.4), channel_id=1, source_target_pairs={{0,8},{8,16},{16,24},{24,32},{32,40},{40,48},{48,56},{56,64},{64,7... | collective-permute-start | bytes 2359304 | tf_op jit(solution)/shard_map/ppermute | solution.py:17
  46.5 201.5 %collective-permute-start.1 = (bf16[2,256,768]{2,1,0:T(8,128)(2,1)}, bf16[2,256,768]{2,1,0:T(8,128)(2,1)}, u32[]{:S(2)}, u32[]{:S(2)}) collective-permute-start(bf16[2,256,768]{2,1,0:T(8,128)(2,1)} %pad_maximum_fusion.4), channel_id=1, source_target_pairs={{8,0},{16,8},{24,16},{32,24},{40,32},{48,40},{56,48},{64,56},{72,6... | collective-permute-start | bytes 2359304 | tf_op jit(solution)/shard_map/ppermute | solution.py:20
  266.1 1.8 copy-start.3
  266.6 1.3 copy-start.1
  270.3 1.5 copy-start.2
  270.3 2.0 copy-start.4
  270.3 2.2 copy-start.7
  273.8 0.9 copy-start.8
  289.9 1.8 copy-start.3
  290.4 1.3 copy-start.1
  294.1 1.5 copy-start.2
  294.1 2.0 copy-start.4
  294.1 2.2 copy-start.7
  297.6 0.9 copy-start.8
where the time goes:
time: 330 us; the launch traced here: 328 us
  waiting for transfers between devices  153 us (46%)
  starting transfers between devices  65 us (20%)
  local copies, waits for them, and re-layouts  54.7 us (17%)
  blocking collectives  27.2 us (8%)
  other arithmetic  18.8 us (6%)
  loops' own time  5.72 us (2%)
  matrix products  3.93 us (1%)
    ppermute x2, waiting for transfers between devices, with_halo(): lax.ppermute(lax.slice_in_dim(block, 0, width, axis=dim), axis, backward)  129 us
    ppermute x2, starting transfers between devices, with_halo(): lax.ppermute(lax.slice_in_dim(block, 0, width, axis=dim), axis, backward)  47.6 us
    all_to_all x1, blocking collectives, local(): lax.all_to_all(gated, 'head', split_axis=0, concat_axis=1, tiled=True)  27.2 us
    ppermute x2, waiting for transfers between devices, with_halo(): lax.ppermute(lax.slice_in_dim(block, block.shape[dim] - width, None, axis...  13.2 us
    reshape x1, local copies, waits for them, and re-layouts, local(): widened = widened.reshape(2, 3 * cache_tiles, TILE, heads_here, HD)  10.8 us
    all_to_all x1, waiting for transfers between devices, local(): lax.all_to_all(keys, 'head', split_axis=1, concat_axis=0, tiled=True)  10.7 us
    reshape x4, local copies, waits for them, and re-layouts, group_blocks(): return window.reshape(2, 5, TILE, heads_here, HD)  9.41 us
    concatenate x2, other arithmetic, with_halo(): block = jnp.concatenate([low, block, high], axis=dim)  7.87 us
  transfers between devices with their start and end apart: 7, of which 3 were waited for; matrix products, arithmetic and copies ran while one was open for 9% of the time, Pallas kernels for 0%

commit v1 on v0

--- a/solution.py
+++ b/solution.py
@@ -1,3 +1,4 @@
+import functools
 import jax
 import jax.numpy as jnp
 from jax import lax
@@ -7,6 +8,19 @@
 TILE = 128
 REACH = 4
 NEGATIVE = -1e30
+
+
+def wait_the_circles(shard_in, which_dim, dim_i):
+    step_out = jnp.concatenate(
+        lax.all_to_all(
+            jnp.stack(jnp.split(shard_in, lax.axis_size("head"), axis=which_dim)), "head", 0, 0
+        ),
+        axis=dim_i,
+    )
+    return step_out
+
+
+trace_rounds = functools.partial(wait_the_circles, which_dim=1, dim_i=0)
 
 
 def with_halo(block, sides, width):
@@ -50,7 +64,7 @@
 def local(queries, keys, values, cache_keys, cache_values, pattern, reached, gate):
     local_q, local_k, local_v = (
         lax.all_to_all(queries, "head", split_axis=1, concat_axis=0, tiled=True),
-        lax.all_to_all(keys, "head", split_axis=1, concat_axis=0, tiled=True),
+        trace_rounds(keys),
         lax.all_to_all(values, "head", split_axis=1, concat_axis=0, tiled=True),
     )
     rows = local_q.shape[0]

time: 330 us -> 340 us (1.030)
  local copies, waits for them, and re-layouts: 54.7 us -> 64.3 us
    unnamed x12 -> x19, local copies, waits for them, and re-layouts: 6.55 us -> 16.6 us
where the time goes in v1:
time: 340 us; the launch traced here: 338 us
  waiting for transfers between devices  153 us (45%)
  starting transfers between devices  65 us (19%)
  local copies, waits for them, and re-layouts  64.3 us (19%)
  blocking collectives  27.2 us (8%)
  other arithmetic  18.8 us (6%)
  loops' own time  5.72 us (2%)
  matrix products  3.93 us (1%)
    ppermute x2, waiting for transfers between devices, with_halo(): lax.ppermute(lax.slice_in_dim(block, 0, width, axis=dim), axis, backward)  129 us
    ppermute x2, starting transfers between devices, with_halo(): lax.ppermute(lax.slice_in_dim(block, 0, width, axis=dim), axis, backward)  47.6 us
    all_to_all x1, blocking collectives, local(): lax.all_to_all(gated, 'head', split_axis=0, concat_axis=1, tiled=True)  27.2 us
    unnamed x19, local copies, waits for them, and re-layouts  16.6 us
    ppermute x2, waiting for transfers between devices, with_halo(): lax.ppermute(lax.slice_in_dim(block, block.shape[dim] - width, None, axis...  13.2 us
    reshape x1, local copies, waits for them, and re-layouts, local(): widened = widened.reshape(2, 3 * cache_tiles, TILE, heads_here, HD)  10.8 us
    all_to_all x1, waiting for transfers between devices, wait_the_circles(): lax.all_to_all(jnp.stack(jnp.split(shard_in, lax.axis_size('head'), axis=...  10.7 us
    reshape x4, local copies, waits for them, and re-layouts, group_blocks(): return window.reshape(2, 5, TILE, heads_here, HD)  9.41 us
  transfers between devices with their start and end apart: 7, of which 3 were waited for; matrix products, arithmetic and copies ran while one was open for 9% of the time, Pallas kernels for 0%

profile of v1, /device:TPU:256, one launch (start us, length us, event | category | flops | bytes accessed | tf_op | source)
XLA Modules:
  0.0 337.9 jit_solution(13195144934840607314)
XLA Ops:
  0.0 1.6 bitcast_dynamic-update-slice_fusion.9
  11.5 3.6 %all-to-all-start = ((bf16[8,32,768]{2,1,0:T(8,128)(2,1)}), bf16[8,32,768]{2,1,0:T(8,128)(2,1)S(1)}, u32[]{:S(2)}, u32[]{:S(2)}) async-start(bf16[8,32,768]{2,1,0:T(8,128)(2,1)} %bitcast_dynamic-update-slice_fusion.2), calls=%async_computation | async-start | bytes 786432 | tf_op jit(solution)/shard_map/all_to_all | solution.py:15
  15.1 1.8 copy.74
  16.9 10.7 %all-to-all-done = bf16[8,32,768]{2,1,0:T(8,128)(2,1)S(1)} async-done(((bf16[8,32,768]{2,1,0:T(8,128)(2,1)}), bf16[8,32,768]{2,1,0:T(8,128)(2,1)S(1)}, u32[]{:S(2)}, u32[]{:S(2)}) %all-to-all-start) | async-done | bytes 393248 | tf_op jit(solution)/shard_map/all_to_all | solution.py:15
  27.5 3.5 %all-to-all-start.1 = ((bf16[32,8,768]{2,0,1:T(8,128)(2,1)}), bf16[32,8,768]{2,0,1:T(8,128)(2,1)S(1)}, u32[]{:S(2)}, u32[]{:S(2)}) async-start(bf16[32,8,768]{2,0,1:T(8,128)(2,1)} %bitcast.80), calls=%async_computation.1 | async-start | bytes 786432 | tf_op jit(solution)/shard_map/all_to_all | solution.py:68
  32.3 3.5 %collective-permute-start.2 = (bf16[2,512,768]{2,1,0:T(8,128)(2,1)}, bf16[2,512,768]{2,1,0:T(8,128)(2,1)}, u32[]{:S(2)}, u32[]{:S(2)}) collective-permute-start(bf16[2,512,768]{2,1,0:T(8,128)(2,1)} %pad_maximum_fusion.3), channel_id=1, source_target_pairs={{0,8},{8,16},{16,24},{24,32},{32,40},{40,48},{48,56},{56,64},{64,7... | collective-permute-start | bytes 4718600 | tf_op jit(solution)/shard_map/ppermute | solution.py:31
  35.8 10.5 %collective-permute-start.3 = (bf16[2,512,768]{2,1,0:T(8,128)(2,1)}, bf16[2,512,768]{2,1,0:T(8,128)(2,1)}, u32[]{:S(2)}, u32[]{:S(2)}) collective-permute-start(bf16[2,512,768]{2,1,0:T(8,128)(2,1)} %pad_maximum_fusion.3), channel_id=1, source_target_pairs={{8,0},{16,8},{24,16},{32,24},{40,32},{48,40},{56,48},{64,56},{72,6... | collective-permute-start | bytes 4718600 | tf_op jit(solution)/shard_map/ppermute | solution.py:34
  47.1 5.0 %all-to-all-start.2 = ((bf16[32,8,768]{2,0,1:T(8,128)(2,1)}), bf16[32,8,768]{2,0,1:T(8,128)(2,1)S(1)}, u32[]{:S(2)}, u32[]{:S(2)}) async-start(bf16[32,8,768]{2,0,1:T(8,128)(2,1)} %bitcast.79), calls=%async_computation.2 | async-start | bytes 786432 | tf_op jit(solution)/shard_map/all_to_all | solution.py:66
  54.1 1.9 collective-permute-start
  56.0 37.1 %collective-permute-start.1 = (bf16[2,256,768]{2,1,0:T(8,128)(2,1)}, bf16[2,256,768]{2,1,0:T(8,128)(2,1)}, u32[]{:S(2)}, u32[]{:S(2)}) collective-permute-start(bf16[2,256,768]{2,1,0:T(8,128)(2,1)} %pad_maximum_fusion.4), channel_id=1, source_target_pairs={{8,0},{16,8},{24,16},{32,24},{40,32},{48,40},{56,48},{64,56},{72,6... | collective-permute-start | bytes 2359304 | tf_op jit(solution)/shard_map/ppermute | solution.py:34
  93.2 128.9 %collective-permute-done.3 = bf16[2,512,768]{2,1,0:T(8,128)(2,1)} collective-permute-done((bf16[2,512,768]{2,1,0:T(8,128)(2,1)}, bf16[2,512,768]{2,1,0:T(8,128)(2,1)}, u32[]{:S(2)}, u32[]{:S(2)}) %collective-permute-start.3) | collective-permute-done | bytes 1572896 | tf_op jit(solution)/shard_map/ppermute | solution.py:34
  222.2 4.9 %pad_maximum_fusion.1 = bf16[2,1536,768]{2,1,0:T(8,128)(2,1)} fusion(bf16[2,512,768]{2,1,0:T(8,128)(2,1)} %collective-permute-done.3, bf16[1,512,768]{2,1,0:T(8,128)(2,1)S(1)} %bitcast.122, bf16[1,512,768]{2,1,0:T(8,128)(2,1)S(1)} %bitcast.124, bf16[2,512,768]{2,1,0:T(8,128)(2,1)} %collective-permute-done.2), kind=kLoop, calls=%fused_computation.38 | loop fusion | flops 18874368 | bytes 9437184 | tf_op jit(solution)/shard_map/concatenate | solution.py:35
  227.1 10.8 %reshape.78 = bf16[2,12,128,6,128]{4,3,2,1,0:T(8,128)(2,1)} reshape(bf16[2,1536,768]{2,1,0:T(8,128)(2,1)} %pad_maximum_fusion.1) | data formatting | bytes 9437184 | tf_op jit(solution)/shard_map/reshape | solution.py:98
  237.8 6.4 %copy.55 = bf16[2,12,128,6,128]{4,2,3,1,0:T(8,128)(2,1)} copy(bf16[2,12,128,6,128]{4,3,2,1,0:T(8,128)(2,1)} %reshape.78) | data formatting | bytes 9437184
  244.3 13.2 %collective-permute-done = bf16[2,256,768]{2,1,0:T(8,128)(2,1)} collective-permute-done((bf16[2,256,768]{2,1,0:T(8,128)(2,1)}, bf16[2,256,768]{2,1,0:T(8,128)(2,1)}, u32[]{:S(2)}, u32[]{:S(2)}) %collective-permute-start) | collective-permute-done | bytes 786464 | tf_op jit(solution)/shard_map/ppermute | solution.py:31
  257.5 3.0 pad_maximum_fusion.2
  260.5 47.6 %while.17 = (s32[]{:T(128)}, f32[2,128,6,128]{1,3,2,0:T(8,128)}, f32[2,6,128]{2,1,0:T(8,128)S(1)}, f32[2,6,128]{2,1,0:T(8,128)S(1)}, s32[2]{0:T(128)S(1)}, /*ind...) while((s32[]{:T(128)}, f32[2,128,6,128]{1,3,2,0:T(8,128)}, ...), condition=%wide.region_3.4_spmd.clone, body=%wide.region_0.3_spmd.clone.sunk | while | flops 465272384 | bytes 78874744 | solution.py:107
  263.2 3.2 gather_fusion
  268.5 2.9 constant_dynamic-slice_fusion.6
  271.4 4.2 %reshape.101 = bf16[2,5,128,6,128]{4,3,2,1,0:T(8,128)(2,1)S(1)} reshape(bf16[2,640,768]{2,1,0:T(8,128)(2,1)} %constant_dynamic-slice_fusion.6) | data formatting | bytes 3932160 | tf_op jit(solution)/shard_map/while/body/eval_jaxpr/reshape | solution.py:95
  287.0 3.2 gather_fusion
  292.3 2.9 constant_dynamic-slice_fusion.6
  295.2 4.2 %reshape.101 = bf16[2,5,128,6,128]{4,3,2,1,0:T(8,128)(2,1)S(1)} reshape(bf16[2,640,768]{2,1,0:T(8,128)(2,1)} %constant_dynamic-slice_fusion.6) | data formatting | bytes 3932160 | tf_op jit(solution)/shard_map/while/body/eval_jaxpr/reshape | solution.py:95
  310.0 27.2 %all_to_all.56 = bf16[8,32,768]{2,1,0:T(8,128)(2,1)S(1)} all-to-all(bf16[8,32,768]{2,1,0:T(8,128)(2,1)S(1)} %multiply_convert_fusion), channel_id=1, replica_groups=mesh['ctx'=64,'head'=8] {'head'}, dimensions={0} | all-to-all | bytes 786432 | tf_op jit(solution)/shard_map/all_to_all | solution.py:110
  (101 shorter events, 37.9 us)
Async XLA Ops:
  0.0 52.1 %copy-start = (s32[128,4]{0,1:T(4,128)S(1)}, s32[128,4]{0,1:T(4,128)}, u32[]{:S(2)}) copy-start(s32[128,4]{0,1:T(4,128)} %param.15) | copy-start | bytes 6148
  0.0 31.0 %copy-start.6 = (bf16[512,768]{1,0:T(8,128)(2,1)S(1)}, bf16[512,768]{1,0:T(8,128)(2,1)}, u32[]{:S(2)}) copy-start(bf16[512,768]{1,0:T(8,128)(2,1)} %param.13) | copy-start | bytes 2359300
  0.0 31.0 %copy-start.5 = (bf16[512,768]{1,0:T(8,128)(2,1)S(1)}, bf16[512,768]{1,0:T(8,128)(2,1)}, u32[]{:S(2)}) copy-start(bf16[512,768]{1,0:T(8,128)(2,1)} %param.14) | copy-start | bytes 2359300
  0.0 46.3 %copy-start.9 = (bf16[32,6144]{1,0:T(8,128)(2,1)S(1)}, bf16[32,6144]{1,0:T(8,128)(2,1)}, u32[]{:S(2)}) copy-start(bf16[32,6144]{1,0:T(8,128)(2,1)} %param.10) | copy-start | bytes 1179652
  11.5 40.8 %copy-start.10 = (s32[128]{0:T(128)S(1)}, s32[128]{0:T(128)}, u32[]{:S(2)}) copy-start(s32[128]{0:T(128)} %param.16) | copy-start | bytes 1540
  11.5 16.0 %all-to-all-start = ((bf16[8,32,768]{2,1,0:T(8,128)(2,1)}), bf16[8,32,768]{2,1,0:T(8,128)(2,1)S(1)}, u32[]{:S(2)}, u32[]{:S(2)}) async-start(bf16[8,32,768]{2,1,0:T(8,128)(2,1)} %bitcast_dynamic-update-slice_fusion.2), calls=%async_computation | async-start | bytes 786432 | tf_op jit(solution)/shard_map/all_to_all | solution.py:15
  27.5 19.5 %all-to-all-start.1 = ((bf16[32,8,768]{2,0,1:T(8,128)(2,1)}), bf16[32,8,768]{2,0,1:T(8,128)(2,1)S(1)}, u32[]{:S(2)}, u32[]{:S(2)}) async-start(bf16[32,8,768]{2,0,1:T(8,128)(2,1)} %bitcast.80), calls=%async_computation.1 | async-start | bytes 786432 | tf_op jit(solution)/shard_map/all_to_all | solution.py:68
  32.3 60.9 %collective-permute-start.2 = (bf16[2,512,768]{2,1,0:T(8,128)(2,1)}, bf16[2,512,768]{2,1,0:T(8,128)(2,1)}, u32[]{:S(2)}, u32[]{:S(2)}) collective-permute-start(bf16[2,512,768]{2,1,0:T(8,128)(2,1)} %pad_maximum_fusion.3), channel_id=1, source_target_pairs={{0,8},{8,16},{16,24},{24,32},{32,40},{40,48},{48,56},{56,64},{64,7... | collective-permute-start | bytes 4718600 | tf_op jit(solution)/shard_map/ppermute | solution.py:31
  35.8 186.4 %collective-permute-start.3 = (bf16[2,512,768]{2,1,0:T(8,128)(2,1)}, bf16[2,512,768]{2,1,0:T(8,128)(2,1)}, u32[]{:S(2)}, u32[]{:S(2)}) collective-permute-start(bf16[2,512,768]{2,1,0:T(8,128)(2,1)} %pad_maximum_fusion.3), channel_id=1, source_target_pairs={{8,0},{16,8},{24,16},{32,24},{40,32},{48,40},{56,48},{64,56},{72,6... | collective-permute-start | bytes 4718600 | tf_op jit(solution)/shard_map/ppermute | solution.py:34
  47.1 213.4 %all-to-all-start.2 = ((bf16[32,8,768]{2,0,1:T(8,128)(2,1)}), bf16[32,8,768]{2,0,1:T(8,128)(2,1)S(1)}, u32[]{:S(2)}, u32[]{:S(2)}) async-start(bf16[32,8,768]{2,0,1:T(8,128)(2,1)} %bitcast.79), calls=%async_computation.2 | async-start | bytes 786432 | tf_op jit(solution)/shard_map/all_to_all | solution.py:66
  54.1 203.4 %collective-permute-start = (bf16[2,256,768]{2,1,0:T(8,128)(2,1)}, bf16[2,256,768]{2,1,0:T(8,128)(2,1)}, u32[]{:S(2)}, u32[]{:S(2)}) collective-permute-start(bf16[2,256,768]{2,1,0:T(8,128)(2,1)} %pad_maximum_fusion.4), channel_id=1, source_target_pairs={{0,8},{8,16},{16,24},{24,32},{32,40},{40,48},{48,56},{56,64},{64,7... | collective-permute-start | bytes 2359304 | tf_op jit(solution)/shard_map/ppermute | solution.py:31
  56.0 201.5 %collective-permute-start.1 = (bf16[2,256,768]{2,1,0:T(8,128)(2,1)}, bf16[2,256,768]{2,1,0:T(8,128)(2,1)}, u32[]{:S(2)}, u32[]{:S(2)}) collective-permute-start(bf16[2,256,768]{2,1,0:T(8,128)(2,1)} %pad_maximum_fusion.4), channel_id=1, source_target_pairs={{8,0},{16,8},{24,16},{32,24},{40,32},{48,40},{56,48},{64,56},{72,6... | collective-permute-start | bytes 2359304 | tf_op jit(solution)/shard_map/ppermute | solution.py:34
  275.6 1.8 copy-start.3
  276.2 1.3 copy-start.1
  279.8 1.5 copy-start.2
  279.8 2.0 copy-start.4
  279.8 2.2 copy-start.7
  283.4 0.9 copy-start.8
  299.4 1.8 copy-start.3
  300.0 1.3 copy-start.1
  303.6 1.5 copy-start.2
  303.6 2.0 copy-start.4
  303.6 2.2 copy-start.7
  307.2 0.9 copy-start.8
